TPU v7x, 32 devices: a whole 2x2x4 slice. The times are simulated.
32 devices in a mesh: leaf: 8 (over z, y), row: 2 (over core), col: 2 (over x).
Axes of the slice: x: 2, y: 2, z: 4, core: 2. Of those that a mesh axis runs over, the one named last changes fastest.
Arguments:
- sigma_top: float32 [4096, 4096], P('row', ('leaf', 'col'))
- structure: int32 [8, 16], replicated, may hold values from 0 to 31, as said below
- lower: float32 [8, 2048, 2048], P('leaf', 'row', 'col'), may hold values from -0.25 to 0.25
- dinv: float32 [8, 2048, 2048], P('leaf', 'row', 'col'), may hold values from -6 to 6
Outputs:
- sigma_sj: float32 [8, 2048, 2048], P('leaf', 'row', 'col')
- sigma_jj: float32 [8, 2048, 2048], P('leaf', 'row', 'col')
Inputs may be any that keep to these rules, and one draw needn't show every extreme that they name: `structure`: each row lists 16 distinct tiles in increasing order and always holds tile 0 and tile 32 - 1.
All inputs are finite; a program needn't handle non-finite values.
Results may differ from a plain program's by a relative error of at most 0.0003.
Values sent between devices are 32-bit elements; how exact they have to be, the bound alone decides.
No kernel may reach another device: no remote copies, remote signals or barrier semaphores. Data moves between devices by JAX's collectives and lax.ppermute only.
A program may use at most 192 MiB of HBM per device.

v0:
```python
import jax
import jax.numpy as jnp
from jax import lax
from jax.sharding import PartitionSpec as P

TILE = 128


def body(sigma_top, structure, lower, dinv):
    factor_block = lower[0]
    diag_inverse = dinv[0]
    struct_rows = factor_block.shape[0]
    n_row = lax.axis_size("row")
    n_col = lax.axis_size("col")
    total_rows = struct_rows * n_row
    root_rows = sigma_top.shape[0]
    within = jnp.arange(TILE, dtype=jnp.int32)
    all_indices = (structure[:, :, None] * TILE + within[None, None, :]).reshape(
        structure.shape[0], -1
    )
    leaf_index = lax.axis_index("leaf")
    own_indices = lax.dynamic_index_in_dim(all_indices, leaf_index, 0, keepdims=False)
    first_root_row = lax.axis_index("row") * root_rows
    quarter = total_rows // n_col
    wanted_cols = lax.dynamic_slice_in_dim(own_indices, lax.axis_index("col") * quarter, quarter)
    empty_cols = jnp.zeros((root_rows, quarter), jnp.float32)
    shard_piece = lax.all_gather(sigma_top, ("leaf", "col"), axis=1, tiled=True)
    piece_width = shard_piece.shape[1]
    inside = (wanted_cols >= 0) & (wanted_cols < piece_width)
    values = jnp.take(shard_piece, jnp.clip(wanted_cols, 0, piece_width - 1), axis=1)
    picked_cols = jnp.where(inside[None, :], values, empty_cols)
    wanted = own_indices - first_root_row
    inside = (wanted >= 0) & (wanted < root_rows)
    values = jnp.take(picked_cols, jnp.clip(wanted, 0, root_rows - 1), axis=0)
    sigma_block = lax.psum_scatter(
        jnp.where(inside[:, None], values, 0.0), "row", scatter_dimension=0, tiled=True
    )
    row_panel = lax.all_gather(sigma_block, "col", axis=1, tiled=True)
    cross = -jnp.dot(
        row_panel,
        lax.all_gather(factor_block, "row", axis=0, tiled=True),
        precision=lax.Precision.HIGHEST,
        preferred_element_type=jnp.float32,
    )
    factor_rows = lax.all_gather(factor_block, "col", axis=1, tiled=True)
    front = diag_inverse + lax.psum_scatter(
        -lax.dot_general(
            factor_rows,
            cross,
            (((0,), (0,)), ((), ())),
            precision=lax.Precision.HIGHEST,
            preferred_element_type=jnp.float32,
        ),
        "row",
        scatter_dimension=0,
        tiled=True,
    )
    return (cross[None], front[None])


def solution(mesh):
    placed = (P("row", ("leaf", "col")), P(), P("leaf", "row", "col"), P("leaf", "row", "col"))
    return jax.shard_map(
        body,
        mesh=mesh,
        in_specs=placed,
        out_specs=(P("leaf", "row", "col"), P("leaf", "row", "col")),
        check_vma=False,
    )
```

profile of v0, /device:TPU:0, one launch (start us, length us, event | category | flops | bytes accessed | tf_op | source)
XLA Modules:
  0.0 738.3 jit_solution(9349008275643625200)
XLA Ops:
  7.2 0.0 all-gather.7.cloned.1.call-start
  7.2 2.9 copy.11
  10.1 0.0 reduce-scatter.3.cloned.1.call-start
  10.2 0.7 broadcast_multiply_fusion
  10.9 0.1 copy.10
  10.9 0.1 bitcast_add_fusion.1
  11.0 0.1 and_reduce_fusion.1
  11.1 0.1 and_reduce_fusion
  11.2 0.1 compare_select_fusion.1
  11.4 353.6 %all-gather.7.cloned.1.call-done = f32[2048,4096]{0,1:T(8,128)} async-done(((f32[2048,256]{0,1:T(8,128)}), f32[2048,4096]{0,1:T(8,128)}) %all-gather.7.cloned.1.call-update) | async-done | bytes 33554448 | tf_op jit(solution)/shard_map/all_gather | solution.py:27
  364.9 19.6 %gather_fusion = f32[1024,2048]{1,0:T(8,128)} fusion(f32[2048,4096]{0,1:T(8,128)} %all-gather.7.cloned.1.call-done, s32[1024]{0:T(1024)S(1)} %broadcast_clamp_fusion.2), kind=kCustom, calls=%fused_computation | custom fusion | bytes 16781312 | tf_op jit(solution)/shard_map/jit(_take)/gather | solution.py:30
  384.5 6.2 select_bitcast_fusion
  390.7 9.3 %copy.12 = f32[2048,1024]{1,0:T(8,128)} copy(f32[2048,1024]{0,1:T(8,128)} %select_bitcast_fusion) | data formatting | bytes 16777216 | tf_op jit(solution)/shard_map/jit(_where)/select_n | solution.py:31
  400.0 15.1 %gather_fusion.1 = f32[2048,1024]{1,0:T(8,128)} fusion(f32[2048,1024]{1,0:T(8,128)} %copy.12, s32[2048]{0:T(1024)S(1)} %broadcast_clamp_fusion), kind=kCustom, calls=%fused_computation.1 | custom fusion | bytes 16785408 | tf_op jit(solution)/shard_map/jit(_take)/gather | solution.py:34
  415.1 5.9 select_select_fusion
  421.1 0.0 all-gather.11.cloned.1.call-start
  421.1 0.7 all-gather.11.cloned.1.call-update
  421.8 0.0 all-gather.9.cloned.1.call-start
  421.9 14.4 %reduce-scatter.3.cloned.1.call-done = f32[1024,1024]{1,0:T(8,128)} async-done(((f32[2048,1024]{1,0:T(8,128)}), f32[1024,1024]{1,0:T(8,128)}) %reduce-scatter.3.cloned.1.call-update) | async-done | bytes 4194320 | tf_op jit(solution)/shard_map/reduce_scatter | solution.py:35
  436.2 0.0 all-gather.13.cloned.1.call-start
  436.3 0.5 all-gather.13.cloned.1.call-update
  436.8 0.0 reduce-scatter.5.cloned.1.call-start
  436.9 22.1 %all-gather.11.cloned.1.call-done = f32[1,2048,1024]{2,1,0:T(8,128)} async-done(((f32[1,1024,1024]{2,1,0:T(8,128)}), f32[1,2048,1024]{2,1,0:T(8,128)}) %all-gather.11.cloned.1.call-update) | async-done | bytes 8388624 | tf_op jit(solution)/shard_map/all_gather | solution.py:41
  459.0 106.7 %all-gather.9.cloned.1.call-done = f32[1024,2048]{1,0:T(8,128)} async-done(((f32[1024,1024]{1,0:T(8,128)}), f32[1024,2048]{1,0:T(8,128)}) %all-gather.9.cloned.1.call-update) | async-done | bytes 8388624 | tf_op jit(solution)/shard_map/all_gather | solution.py:38
  565.7 31.8 %fusion.2 = f32[1024,1024]{1,0:T(8,128)} fusion(f32[1024,2048]{1,0:T(8,128)} %all-gather.9.cloned.1.call-done, f32[1,2048,1024]{2,1,0:T(8,128)} %all-gather.11.cloned.1.call-done), kind=kOutput, calls=%fused_computation.4 | convolution fusion | flops 25769803776 | bytes 20971520 | tf_op jit(solution)/shard_map/dot_general | solution.py:39
  597.5 73.7 %all-gather.13.cloned.1.call-done = f32[1,1024,2048]{2,1,0:T(8,128)} async-done(((f32[1,1024,1024]{2,1,0:T(8,128)}), f32[1,1024,2048]{2,1,0:T(8,128)}) %all-gather.13.cloned.1.call-update) | async-done | bytes 8388624 | tf_op jit(solution)/shard_map/all_gather | solution.py:45
  671.2 31.2 %negate_bitcast_fusion = f32[2048,1024]{0,1:T(8,128)} fusion(f32[1,1024,2048]{2,1,0:T(8,128)} %all-gather.13.cloned.1.call-done, f32[1024,1024]{1,0:T(8,128)} %fusion.2), kind=kOutput, calls=%fused_computation.7 | convolution fusion | flops 25772949504 | bytes 20971520 | tf_op jit(solution)/shard_map/dot_general | solution.py:47
  702.4 5.4 copy.13
  707.7 6.1 negate_bitcast_fusion.1
  713.8 5.5 reduce-scatter.5.cloned.1.call-done
  719.3 6.8 fusion.6
  726.1 5.3 copy.14
  (10 shorter events, 0.1 us)
Async XLA Ops:
  7.2 357.8 %all-gather.7.cloned.1.call-start = ((), (), s32[]{:S(2)}) async-start(), calls=%async_computation.2 | async-start | bytes 35651584 | tf_op jit(solution)/shard_map/all_gather | solution.py:27
  10.1 426.1 %reduce-scatter.3.cloned.1.call-start = ((), (), s32[]{:S(2)}) async-start(), calls=%async_computation.3 | async-start | bytes 12582912 | tf_op jit(solution)/shard_map/reduce_scatter | solution.py:35
  421.1 37.9 %all-gather.11.cloned.1.call-start = ((), (), s32[]{:S(2)}) async-start(), calls=%async_computation.6 | async-start | bytes 12582912 | tf_op jit(solution)/shard_map/all_gather | solution.py:41
  421.8 143.9 %all-gather.9.cloned.1.call-start = ((), (), s32[]{:S(2)}) async-start(), calls=%async_computation.4 | async-start | bytes 12582912 | tf_op jit(solution)/shard_map/all_gather | solution.py:38
  436.2 234.9 %all-gather.13.cloned.1.call-start = ((), (), s32[]{:S(2)}) async-start(), calls=%async_computation.7 | async-start | bytes 12582912 | tf_op jit(solution)/shard_map/all_gather | solution.py:45
  436.8 282.5 %reduce-scatter.5.cloned.1.call-start = ((), (), s32[]{:S(2)}) async-start(), calls=%async_computation.5 | async-start | bytes 12582912 | tf_op jit(solution)/shard_map/reduce_scatter | solution.py:46
Sparse Core Ops, SparseCore 0:
  11.3 353.5 all-gather.6
  421.2 14.9 reduce-scatter.2
  437.8 21.1 all-gather.10
  460.5 105.1 all-gather.8
  567.1 103.9 all-gather.12
  702.5 16.7 reduce-scatter.4
where the time goes:
time: 739 us; the launch traced here: 738 us
  waiting for transfers between devices  577 us (78%)
  matrix products  63 us (9%)
  local copies, waits for them, and re-layouts  57.6 us (8%)
  other arithmetic  26.1 us (4%)
  between operations  14.2 us (2%)
    all_gather x1, waiting for transfers between devices, body(): shard_piece = lax.all_gather(sigma_top, ('leaf', 'col'), axis=1, tiled=True)  354 us
    all_gather x1, waiting for transfers between devices, body(): row_panel = lax.all_gather(sigma_block, 'col', axis=1, tiled=True)  107 us
    all_gather x1, waiting for transfers between devices, body(): factor_rows = lax.all_gather(factor_block, 'col', axis=1, tiled=True)  73.7 us
    dot_general x1, matrix products, body(): jnp.dot(row_panel, lax.all_gather(factor_block, 'row', axis=0, tiled=True...  31.8 us
    dot_general x1, matrix products, body(): lax.dot_general(factor_rows, cross, (((0,), (0,)), ((), ())), precision=l...  31.2 us
    all_gather x1, waiting for transfers between devices, body(): lax.all_gather(factor_block, 'row', axis=0, tiled=True)  22.1 us
    gather x1, local copies, waits for them, and re-layouts, body(): jnp.take(shard_piece, jnp.clip(wanted_cols, 0, piece_width - 1), axis=1)  19.6 us
    gather x1, local copies, waits for them, and re-layouts, body(): values = jnp.take(picked_cols, jnp.clip(wanted, 0, root_rows - 1), axis=0)  15.1 us
  transfers between devices with their start and end apart: 6, of which 6 were waited for; matrix products, arithmetic and copies ran while one was open for 6% of the time, Pallas kernels for 0%

commit v1 on v0

--- a/solution.py
+++ b/solution.py
@@ -42,7 +42,15 @@
         precision=lax.Precision.HIGHEST,
         preferred_element_type=jnp.float32,
     )
-    factor_rows = lax.all_gather(factor_block, "col", axis=1, tiled=True)
+    ways, here = (lax.axis_size("col"), lax.axis_index("col"))
+    grown, reach = (factor_block, 1)
+    while reach < ways:
+        theirs = lax.ppermute(grown, "col", [(d, d ^ reach) for d in range(ways)])
+        mine_first = jnp.concatenate([grown, theirs], axis=1)
+        theirs_first = jnp.concatenate([theirs, grown], axis=1)
+        grown = jnp.where(here & reach == 0, mine_first, theirs_first)
+        reach = 2 * reach
+    factor_rows = grown
     front = diag_inverse + lax.psum_scatter(
         -lax.dot_general(
             factor_rows,

time: 739 us -> 714 us (0.966)
  waiting for transfers between devices: 577 us -> 563 us
  local copies, waits for them, and re-layouts: 57.6 us -> 48.9 us
    all_gather x1 -> x0, waiting for transfers between devices: 73.7 us -> none  [body(): factor_rows = lax.all_gather(factor_block, 'col', axis=1, tiled=True)]
    all_gather x1, waiting for transfers between devices: 107 us -> 160 us  [body(): row_panel = lax.all_gather(sigma_block, 'col', axis=1, tiled=True)]
    unnamed x3 -> x5, local copies, waits for them, and re-layouts: 13.6 us -> 4.89 us
    reduce_scatter x1, waiting for transfers between devices: 5.49 us -> 13.1 us  [body(): lax.psum_scatter(-lax.dot_general(factor_rows, cross, (((0,), (0,)), ((),...]
  transfers between devices with their start and end apart: 6 -> 6, of which waited for: 6 -> 5; matrix products, arithmetic and copies ran while one was open for 6% -> 5% of each run, Pallas kernels for 0% -> 0%
where the time goes in v1:
time: 714 us
  waiting for transfers between devices  563 us (79%)
  matrix products  60.9 us (9%)
  local copies, waits for them, and re-layouts  48.9 us (7%)
  other arithmetic  25.1 us (4%)
  between operations  13.9 us (2%)
    all_gather x1, waiting for transfers between devices, body(): shard_piece = lax.all_gather(sigma_top, ('leaf', 'col'), axis=1, tiled=True)  354 us
    all_gather x1, waiting for transfers between devices, body(): row_panel = lax.all_gather(sigma_block, 'col', axis=1, tiled=True)  160 us
    dot_general x1, matrix products, body(): lax.dot_general(factor_rows, cross, (((0,), (0,)), ((), ())), precision=l...  31 us
    dot_general x1, matrix products, body(): jnp.dot(row_panel, lax.all_gather(factor_block, 'row', axis=0, tiled=True...  29.9 us
    all_gather x1, waiting for transfers between devices, body(): lax.all_gather(factor_block, 'row', axis=0, tiled=True)  20.8 us
    gather x1, local copies, waits for them, and re-layouts, body(): jnp.take(shard_piece, jnp.clip(wanted_cols, 0, piece_width - 1), axis=1)  19.6 us
    gather x1, local copies, waits for them, and re-layouts, body(): values = jnp.take(picked_cols, jnp.clip(wanted, 0, root_rows - 1), axis=0)  15.1 us
    reduce_scatter x1, waiting for transfers between devices, body(): lax.psum_scatter(jnp.where(inside[:, None], values, 0.0), 'row', scatter_...  14.4 us
  transfers between devices with their start and end apart: 6, of which 5 were waited for; matrix products, arithmetic and copies ran while one was open for 5% of the time, Pallas kernels for 0%

profile of v1, /device:TPU:0, one launch (start us, length us, event | category | flops | bytes accessed | tf_op | source)
XLA Modules:
  0.0 714.0 jit_solution(5489871801818853892)
XLA Ops:
  7.2 0.0 all-gather.5.cloned.1.call-start
  7.2 2.9 copy.9
  10.1 0.0 all-gather.5.cloned.1.call-update
  10.1 0.0 reduce-scatter.3.cloned.1.call-start
  10.2 0.7 broadcast_multiply_fusion
  10.9 0.1 copy.8
  11.0 0.1 bitcast_add_fusion.1
  11.0 0.1 and_reduce_fusion.1
  11.1 0.1 and_reduce_fusion
  11.2 0.1 compare_select_fusion.1
  11.4 353.6 %all-gather.5.cloned.1.call-done = f32[2048,4096]{0,1:T(8,128)} async-done(((f32[2048,256]{0,1:T(8,128)}), f32[2048,4096]{0,1:T(8,128)}) %all-gather.5.cloned.1.call-update) | async-done | bytes 33554448 | tf_op jit(solution)/shard_map/all_gather | solution.py:27
  364.9 19.6 %gather_fusion = f32[1024,2048]{1,0:T(8,128)} fusion(f32[2048,4096]{0,1:T(8,128)} %all-gather.5.cloned.1.call-done, s32[1024]{0:T(1024)S(1)} %broadcast_clamp_fusion.2), kind=kCustom, calls=%fused_computation | custom fusion | bytes 16781312 | tf_op jit(solution)/shard_map/jit(_take)/gather | solution.py:30
  384.5 6.2 select_bitcast_fusion
  390.7 9.3 %copy.10 = f32[2048,1024]{1,0:T(8,128)} copy(f32[2048,1024]{0,1:T(8,128)} %select_bitcast_fusion) | data formatting | bytes 16777216 | tf_op jit(solution)/shard_map/jit(_where)/select_n | solution.py:31
  400.0 15.1 %gather_fusion.1 = f32[2048,1024]{1,0:T(8,128)} fusion(f32[2048,1024]{1,0:T(8,128)} %copy.10, s32[2048]{0:T(1024)S(1)} %broadcast_clamp_fusion), kind=kCustom, calls=%fused_computation.1 | custom fusion | bytes 16785408 | tf_op jit(solution)/shard_map/jit(_take)/gather | solution.py:34
  415.1 5.9 select_select_fusion
  421.0 0.0 reduce-scatter.3.cloned.1.call-update
  421.1 0.0 all-gather.9.cloned.1.call-start
  421.1 0.7 all-gather.9.cloned.1.call-update
  421.8 0.0 all-gather.7.cloned.1.call-start
  421.9 14.4 %reduce-scatter.3.cloned.1.call-done = f32[1024,1024]{1,0:T(8,128)} async-done(((f32[2048,1024]{1,0:T(8,128)}), f32[1024,1024]{1,0:T(8,128)}) %reduce-scatter.3.cloned.1.call-update) | async-done | bytes 4194320 | tf_op jit(solution)/shard_map/reduce_scatter | solution.py:35
  436.2 0.0 all-gather.7.cloned.1.call-update
  436.2 0.0 reduce-scatter.5.cloned.1.call-start
  436.3 1.9 collective-permute-start
  438.2 20.8 %all-gather.9.cloned.1.call-done = f32[1,2048,1024]{2,1,0:T(8,128)} async-done(((f32[1,1024,1024]{2,1,0:T(8,128)}), f32[1,2048,1024]{2,1,0:T(8,128)}) %all-gather.9.cloned.1.call-update) | async-done | bytes 8388624 | tf_op jit(solution)/shard_map/all_gather | solution.py:41
  459.0 160.5 %all-gather.7.cloned.1.call-done = f32[1024,2048]{1,0:T(8,128)} async-done(((f32[1024,1024]{1,0:T(8,128)}), f32[1024,2048]{1,0:T(8,128)}) %all-gather.7.cloned.1.call-update) | async-done | bytes 8388624 | tf_op jit(solution)/shard_map/all_gather | solution.py:38
  619.5 29.9 %fusion.6 = f32[1024,1024]{1,0:T(8,128)S(1)} fusion(f32[1024,2048]{1,0:T(8,128)} %all-gather.7.cloned.1.call-done, f32[1,2048,1024]{2,1,0:T(8,128)} %all-gather.9.cloned.1.call-done), kind=kOutput, calls=%fused_computation.9 | convolution fusion | flops 25769803776 | bytes 20971520 | tf_op jit(solution)/shard_map/dot_general | solution.py:39
  649.4 2.0 copy-done.1
  651.4 31.0 %fusion.10 = f32[2048,1024]{1,0:T(8,128)} fusion(f32[1024,1024]{1,0:T(8,128)} %collective-permute-done, f32[1024,1024]{1,0:T(8,128)S(1)} %bitcast.28, pred[]{:T(512)S(6)} %eq.3, f32[1024,1024]{1,0:T(8,128)S(1)} %fusion.6), kind=kOutput, calls=%fused_computation.16 | convolution fusion | flops 25779240960 | bytes 20971520 | tf_op jit(solution)/shard_map/dot_general | solution.py:55
  682.5 5.0 negate_bitcast_fusion
  687.5 13.1 %reduce-scatter.5.cloned.1.call-done = f32[1024,1024]{1,0:T(8,128)} async-done(((f32[2048,1024]{1,0:T(8,128)}), f32[1024,1024]{1,0:T(8,128)}) %reduce-scatter.5.cloned.1.call-update) | async-done | bytes 4194320 | tf_op jit(solution)/shard_map/reduce_scatter | solution.py:54
  700.6 6.8 fusion.8
  (11 shorter events, 0.1 us)
Async XLA Ops:
  7.2 357.8 %all-gather.5.cloned.1.call-start = ((), (), s32[]{:S(2)}) async-start(), calls=%async_computation.2 | async-start | bytes 35651584 | tf_op jit(solution)/shard_map/all_gather | solution.py:27
  10.1 426.1 %reduce-scatter.3.cloned.1.call-start = ((), (), s32[]{:S(2)}) async-start(), calls=%async_computation.3 | async-start | bytes 12582912 | tf_op jit(solution)/shard_map/reduce_scatter | solution.py:35
  421.1 37.9 %all-gather.9.cloned.1.call-start = ((), (), s32[]{:S(2)}) async-start(), calls=%async_computation.6 | async-start | bytes 12582912 | tf_op jit(solution)/shard_map/all_gather | solution.py:41
  421.8 197.7 %all-gather.7.cloned.1.call-start = ((), (), s32[]{:S(2)}) async-start(), calls=%async_computation.4 | async-start | bytes 12582912 | tf_op jit(solution)/shard_map/all_gather | solution.py:38
  436.2 264.4 %reduce-scatter.5.cloned.1.call-start = ((), (), s32[]{:S(2)}) async-start(), calls=%async_computation.5 | async-start | bytes 12582912 | tf_op jit(solution)/shard_map/reduce_scatter | solution.py:54
  436.3 213.1 %collective-permute-start = (f32[1024,1024]{1,0:T(8,128)}, f32[1024,1024]{1,0:T(8,128)}, u32[]{:S(2)}, u32[]{:S(2)}) collective-permute-start(f32[1024,1024]{1,0:T(8,128)} %bitcast.27), channel_id=1, source_target_pairs={{0,1},{1,0},{2,3},{3,2},{4,5},{5,4},{6,7},{7,6},{8,9},{9,8},{10,11... | collective-permute-start | bytes 12582920 | tf_op jit(solution)/shard_map/ppermute | solution.py:48
  619.5 32.0 %copy-start = (f32[1,1024,1024]{2,1,0:T(8,128)S(1)}, f32[1,1024,1024]{2,1,0:T(8,128)}, u32[]{:S(2)}) copy-start(f32[1,1024,1024]{2,1,0:T(8,128)} %param.6) | copy-start | bytes 12582916
  649.4 2.0 copy-start.1
Sparse Core Ops, SparseCore 0:
  11.3 353.5 all-gather.4
  421.2 14.9 reduce-scatter.2
  437.8 21.1 all-gather.8
  460.5 158.9 all-gather.6
  682.6 17.9 reduce-scatter.4
